TPU v7x, 128 devices: a whole 4x4x4 slice. The times are simulated.
128 devices in a mesh: section: 4 (over z_lo, core), dp: 8 (over x, z_hi), mp: 4 (over y).
Axes of the slice: x: 4, y: 4, z: 4 (z_hi: 2, z_lo: 2; z = z_hi * 2 + z_lo), core: 2. Of those that a mesh axis runs over, the one named last changes fastest.
Arguments:
- entrance: bfloat16 [8, 2, 96, 4096], P('dp'), may hold values from -6 to 6
- lengths: int32 [8, 2], P('dp'), may hold values from 24 to 96
- positives: int32 [8], replicated, may hold values from 0 to 7, each once
- norm_gains: float32 [4, 4096], P('section'), may hold values from 0.5 to 1.5
- query_proj: bfloat16 [4, 4096, 2048], P('section', None, 'mp'), may hold values from -0.09375 to 0.09375
- key_proj: bfloat16 [4, 4096, 512], P('section', None, 'mp'), may hold values from -0.09375 to 0.09375
- value_proj: bfloat16 [4, 4096, 512], P('section', None, 'mp'), may hold values from -0.09375 to 0.09375
- out_proj: bfloat16 [4, 2048, 4096], P('section', 'mp'), may hold values from -0.125 to 0.125
Outputs:
- losses: float32 [4, 7], P('section')
- norm_gain_grad: float32 [4, 4096], P('section', ('dp', 'mp'))
- query_proj_grad: float32 [4, 4096, 2048], P('section', 'dp', 'mp')
- key_proj_grad: float32 [4, 4096, 512], P('section', 'dp', 'mp')
- value_proj_grad: float32 [4, 4096, 512], P('section', 'dp', 'mp')
- out_proj_grad: float32 [4, 2048, 4096], P('section', 'mp', 'dp')
Inputs may be any that keep to these rules, and one draw needn't show every extreme that they name: positives is a permutation of the pair indices. `lengths`: tokens at or past a sequence's length are padding.
All inputs are finite; a program needn't handle non-finite values.
Results may differ from a plain program's by a relative error of at most 0.039.
Values may be sent and summed in bfloat16 or wider, within the bound.
No kernel may reach another device: no remote copies, remote signals or barrier semaphores. Data moves between devices by JAX's collectives and lax.ppermute only.
A program may use at most 128 MiB of HBM per device.

v0:
```python
import jax
import jax.numpy as jnp
from jax import lax
from jax.sharding import PartitionSpec as P

HEAD = 128
WIDTHS = 7
EPSILON = 1e-05
SOFTMAX_TEMPER = 0.05
ROPE_BASE = 500000.0


def passed_along(value, axis, steps):
    count = lax.axis_size(axis)
    first, last = (max(0, -steps), min(count, count - steps))
    return lax.ppermute(value, axis, [(source, source + steps) for source in range(first, last)])


def split_up(array, dim, length):
    before, after = (array.shape[:dim], array.shape[dim + 1 :])
    return jnp.moveaxis(array.reshape(*before, length, -1, *after), dim, 0)


def summed_on_arrival(array, axis, dim):
    length = lax.axis_size(axis)
    pieces = lax.all_to_all(split_up(array, dim, length), axis, 0, 0, tiled=True)
    return jnp.sum(pieces, axis=0)


def edges_of(length, count):
    unit = 8 if length >= 8 * count else 1
    return [length // unit * k // count * unit for k in range(1, count)]


def joined_along(pieces, dim):
    pieces = jnp.moveaxis(pieces, 0, dim)
    dims = pieces.shape
    return pieces.reshape(*dims[:dim], dims[dim] * dims[dim + 1], *dims[dim + 2 :])


def exchange_in_pieces(array, axis, pieces, split_dim, concat_dim):
    blocks = split_up(array, split_dim, lax.axis_size(axis))
    cut = max(range(1, max(2, blocks.ndim - 1)), key=lambda d: blocks.shape[d])
    outs = []
    for piece in jnp.split(blocks, edges_of(blocks.shape[cut], pieces), axis=cut):
        if piece.size:
            outs.append(lax.all_to_all(piece, axis, split_axis=0, concat_axis=0, tiled=True))
    return joined_along(jnp.concatenate(outs, axis=cut), concat_dim)


def sent_together(arrays, axis, dim, along):
    ends, at = ([], 0)
    for a in arrays[:-1]:
        at += a.shape[along]
        ends.append(at)
    both = jnp.concatenate(arrays, axis=along)
    return tuple(jnp.split(lax.all_gather(both, axis, axis=dim, tiled=True), ends, axis=along))


def rope_tables(length, head_size):
    half_size = head_size // 2
    inverse_freq = ROPE_BASE ** (-jnp.arange(half_size, dtype=jnp.float32) * 2.0 / head_size)
    angles = jnp.arange(length, dtype=jnp.float32)[:, None] * inverse_freq[None, :]
    return (jnp.cos(angles), jnp.sin(angles))


def rotate(values, cosine, sine_table):
    half_size = values.shape[-1] // 2
    first_half = values[..., :half_size]
    second = values[..., half_size:]
    cosine = cosine[None, :, None, :]
    sine_table = sine_table[None, :, None, :]
    return jnp.concatenate(
        [first_half * cosine - second * sine_table, second * cosine + first_half * sine_table],
        axis=-1,
    )


def attend(query_pre, key_pre, value_pre):
    seq_count, length, query_width = query_pre.shape
    query_heads = query_width // HEAD
    kv_heads = key_pre.shape[-1] // HEAD
    group_size = query_heads // kv_heads
    cosine, sine_table = rope_tables(length, HEAD)
    query_vectors = rotate(
        query_pre.reshape(seq_count, length, query_heads, HEAD), cosine, sine_table
    ).astype(jnp.bfloat16)
    key_rows = rotate(
        key_pre.reshape(seq_count, length, kv_heads, HEAD), cosine, sine_table
    ).astype(jnp.bfloat16)
    values = value_pre.reshape(seq_count, length, kv_heads, HEAD).astype(jnp.bfloat16)
    query_vectors = query_vectors.reshape(seq_count, length, kv_heads, group_size, HEAD)
    scores = jnp.einsum(
        "sikge,sjke->skgij", query_vectors.astype(jnp.float32), key_rows.astype(jnp.float32)
    ) * HEAD ** (-0.5)
    causal = (
        jnp.arange(length, dtype=jnp.int32)[:, None] >= jnp.arange(length, dtype=jnp.int32)[None, :]
    )
    scores = jnp.where(causal, scores, -1e30)
    weights = jax.nn.softmax(scores, axis=-1).astype(jnp.bfloat16)
    mixture = jnp.einsum(
        "skgij,sjke->sikge", weights.astype(jnp.float32), values.astype(jnp.float32)
    )
    return mixture.reshape(seq_count, length, query_heads * HEAD)


def normalize(hidden_f, gain_vector):
    inv_rms = lax.rsqrt(jnp.mean(hidden_f * hidden_f, axis=-1, keepdims=True) + EPSILON)
    return hidden_f * inv_rms * gain_vector


def contract_rows(left, right):
    return lax.dot_general(
        left, right, (((0,), (0,)), ((), ())), preferred_element_type=jnp.float32
    )


def contract_last(left, right):
    return lax.dot_general(
        left, right, (((left.ndim - 1,), (1,)), ((), ())), preferred_element_type=jnp.float32
    )


def pool_exits(batch_rows, mask_of_valid, counts):
    total_value = jnp.einsum("ki,kiu->ku", mask_of_valid, batch_rows.astype(jnp.float32))
    return total_value / counts[:, None]


def spread_grad(exit_grad, mask_of_valid, counts):
    return mask_of_valid[:, :, None] * (exit_grad / counts[:, None])[:, None, :]


def matryoshka_losses(pooled, positives):
    pair_total = pooled.shape[0]
    target = (jnp.arange(pair_total, dtype=jnp.int32)[None, :] == positives[:, None]).astype(
        jnp.float32
    )
    losses = []
    for level_index in range(WIDTHS):
        leading_width = pooled.shape[-1] // 2**level_index
        query_vectors = pooled[:, 0, :leading_width]
        passage_rows = pooled[:, 1, :leading_width]
        query_vectors = query_vectors * lax.rsqrt(
            jnp.mean(query_vectors * query_vectors, axis=-1, keepdims=True) + 1e-06
        )
        passage_rows = passage_rows * lax.rsqrt(
            jnp.mean(passage_rows * passage_rows, axis=-1, keepdims=True) + 1e-06
        )
        score_matrix = jnp.dot(query_vectors, passage_rows.T, precision=lax.Precision.HIGHEST) / (
            leading_width * SOFTMAX_TEMPER
        )
        picked = jnp.sum(score_matrix * target, axis=-1)
        losses.append(jnp.mean(jax.nn.logsumexp(score_matrix, axis=-1) - picked))
    return jnp.stack(losses)


def pass_along(batch_rows, direction):
    return passed_along(batch_rows, "section", direction)


def forward_section(hidden, gain_vector, query_weight, key_weight, value_weight, out_weight):
    hidden_f = hidden.astype(jnp.float32)
    normed = normalize(hidden_f, gain_vector).astype(jnp.bfloat16)
    mixture = attend(
        jnp.dot(normed, query_weight, preferred_element_type=jnp.float32),
        jnp.dot(normed, key_weight, preferred_element_type=jnp.float32),
        jnp.dot(normed, value_weight, preferred_element_type=jnp.float32),
    ).astype(jnp.bfloat16)
    partial_value = jnp.dot(mixture, out_weight, preferred_element_type=jnp.float32)
    total_value = lax.psum(partial_value.astype(jnp.bfloat16), "mp").astype(jnp.float32)
    return (hidden_f + total_value).astype(jnp.bfloat16)


def backward_section(
    hidden, upstream, gain_vector, query_weight, key_weight, value_weight, out_weight
):
    hidden_f = hidden.astype(jnp.float32)
    inv_rms = lax.rsqrt(jnp.mean(hidden_f * hidden_f, axis=-1, keepdims=True) + EPSILON)
    normed = normalize(hidden_f, gain_vector).astype(jnp.bfloat16)
    out_grad = upstream.astype(jnp.bfloat16)
    mixture_f, pullback = jax.vjp(
        attend,
        jnp.dot(normed, query_weight, preferred_element_type=jnp.float32),
        jnp.dot(normed, key_weight, preferred_element_type=jnp.float32),
        jnp.dot(normed, value_weight, preferred_element_type=jnp.float32),
    )
    mixture = mixture_f.astype(jnp.bfloat16)
    mixture_grad = contract_last(out_grad, out_weight).astype(jnp.bfloat16)
    pulled = pullback(lax.optimization_barrier(mixture_grad).astype(jnp.float32))
    query_grad, key_grad, value_grad = [piece_grad.astype(jnp.bfloat16) for piece_grad in pulled]
    member_grad = (
        contract_last(query_grad, query_weight)
        + contract_last(key_grad, key_weight)
        + contract_last(value_grad, value_weight)
    )
    normed_grad = lax.psum(member_grad.astype(jnp.bfloat16), "mp").astype(jnp.float32)
    rounded = lax.optimization_barrier(member_grad.astype(jnp.bfloat16)).astype(jnp.float32)
    gain_term = jnp.sum(rounded * hidden_f * inv_rms, axis=(0, 1))
    _, norm_pull = jax.vjp(lambda values: normalize(values, gain_vector), hidden_f)
    input_grad = (upstream + norm_pull(normed_grad)[0]).astype(jnp.bfloat16)
    width_all = hidden.shape[-1]
    head_grads = jnp.concatenate([query_grad, key_grad, value_grad], axis=-1)
    stored_now = (
        normed.reshape(-1, width_all),
        out_grad.reshape(-1, width_all),
        head_grads.reshape(-1, head_grads.shape[-1]),
        mixture.reshape(-1, mixture.shape[-1]),
        gain_term,
    )
    return (input_grad, stored_now)


def local(entrance, lengths, positives, norm_gains, query_proj, key_proj, value_proj, out_proj):
    section_count = lax.axis_size("section")
    section_index = lax.axis_index("section")
    pair_count = entrance.shape[0]
    seq_count = 2 * pair_count
    length = entrance.shape[2]
    width_all = entrance.shape[3]
    start_hidden = entrance.reshape(seq_count, length, width_all)
    mask_of_valid = (
        jnp.arange(length, dtype=jnp.int32)[None, :] < lengths.reshape(seq_count, 1)
    ).astype(jnp.float32)
    counts = jnp.sum(mask_of_valid, axis=1)
    gain_vector = norm_gains[0]
    query_weight = query_proj[0]
    key_weight = key_proj[0]
    value_weight = value_proj[0]
    out_weight = out_proj[0]
    current = start_hidden
    saved_input = start_hidden
    exit_rows = start_hidden
    for section_turn in range(section_count):
        produced = forward_section(
            current, gain_vector, query_weight, key_weight, value_weight, out_weight
        )
        chosen = section_index == section_turn
        saved_input = jnp.where(chosen, current, saved_input)
        exit_rows = jnp.where(chosen, produced, exit_rows)
        if section_turn + 1 < section_count:
            arrived = pass_along(produced, 1)
            current = jnp.where(section_index == 0, start_hidden, arrived)
    pooled = pool_exits(exit_rows, mask_of_valid, counts).reshape(pair_count, 2, width_all)
    gathered = lax.all_gather(pooled.astype(jnp.bfloat16), "dp", axis=0, tiled=True).astype(
        pooled.dtype
    )
    losses_now, pullback = jax.vjp(
        lambda embedded: matryoshka_losses(embedded, positives), gathered
    )
    pair_grads = pullback(jnp.ones((WIDTHS,), jnp.float32))[0]
    own_losses = losses_now[None]
    own_grad = lax.dynamic_slice_in_dim(
        pair_grads, lax.axis_index("dp") * pair_count, pair_count, 0
    )
    token_grad = spread_grad(own_grad.reshape(seq_count, width_all), mask_of_valid, counts)
    incoming = jnp.zeros(start_hidden.shape, jnp.bfloat16)
    stored = None
    for section_turn in range(section_count):
        owner_section = section_count - 1 - section_turn
        upstream = token_grad + incoming.astype(jnp.float32)
        input_grad, stored_now = backward_section(
            saved_input, upstream, gain_vector, query_weight, key_weight, value_weight, out_weight
        )
        chosen = section_index == owner_section
        if stored is None:
            stored = stored_now
        else:
            stored = jax.tree.map(
                lambda fresh, former: jnp.where(chosen, fresh, former), stored_now, stored
            )
        if section_turn + 1 < section_count:
            incoming = pass_along(input_grad, -1)
    normed_rows, out_rows, head_grads, mixture_rows, gain_term = stored
    gain_share = summed_on_arrival(gain_term, ("dp", "mp"), 0)
    normed_cols, out_cols = (
        exchange_in_pieces(normed_rows, "dp", 2, 1, 0),
        exchange_in_pieces(out_rows, "dp", 2, 1, 0),
    )
    head_piece, mixture_piece = sent_together((head_grads, mixture_rows), "dp", 0, 1)
    weight_sums = jnp.concatenate(
        [contract_rows(normed_cols, head_piece), contract_rows(out_cols, mixture_piece)], axis=1
    )
    query_cols = query_weight.shape[1]
    kv_cols = key_weight.shape[1]
    query_grad_out = weight_sums[:, :query_cols][None]
    key_grad_out = weight_sums[:, query_cols : query_cols + kv_cols][None]
    value_grad_out = weight_sums[:, query_cols + kv_cols : query_cols + 2 * kv_cols][None]
    out_grad_out = weight_sums[:, query_cols + 2 * kv_cols :].T[None]
    return (
        own_losses,
        gain_share[None],
        query_grad_out,
        key_grad_out,
        value_grad_out,
        out_grad_out,
    )


def solution(mesh):
    in_specs = (
        P("dp", None, None, None),
        P("dp", None),
        P(),
        P("section", None),
        P("section", None, "mp"),
        P("section", None, "mp"),
        P("section", None, "mp"),
        P("section", "mp", None),
    )
    out_specs = (
        P("section", None),
        P("section", ("dp", "mp")),
        P("section", "dp", "mp"),
        P("section", "dp", "mp"),
        P("section", "dp", "mp"),
        P("section", "mp", "dp"),
    )
    return jax.shard_map(local, mesh=mesh, in_specs=in_specs, out_specs=out_specs, check_vma=False)
```

profile of v0, /device:TPU:32, one launch (start us, length us, event | category | flops | bytes accessed | tf_op | source)
XLA Modules:
  0.0 795.2 jit_solution(6946934551017990552)
XLA Ops:
  9.2 6.6 copy.215
  16.0 3.8 fusion.80
  22.3 4.3 convolution_convert_fusion.3
  26.7 52.6 %all-reduce.38.cloned.1.call-done = bf16[2,96,4096]{2,1,0:T(8,128)(2,1)} async-done(((bf16[2,96,4096]{2,1,0:T(8,128)(2,1)}), bf16[2,96,4096]{2,1,0:T(8,128)(2,1)}) %all-reduce.38.cloned.1.call-update) | async-done | bytes 1572880 | tf_op jit(solution)/shard_map/psum | solution.py:170
  79.3 3.1 fusion.25
  84.3 20.1 %collective-permute-done = bf16[2,96,4096]{2,1,0:T(8,128)(2,1)} collective-permute-done((bf16[2,96,4096]{2,1,0:T(8,128)(2,1)}, bf16[2,96,4096]{2,1,0:T(8,128)(2,1)}, u32[]{:S(2)}, u32[]{:S(2)}) %collective-permute-start) | collective-permute-done | bytes 1572896 | tf_op jit(solution)/shard_map/ppermute | solution.py:16
  109.8 2.2 fusion.131
  112.3 4.3 convolution_convert_fusion.2
  116.7 50.4 %all-reduce.40.cloned.1.call-done = bf16[2,96,4096]{2,1,0:T(8,128)(2,1)} async-done(((bf16[2,96,4096]{2,1,0:T(8,128)(2,1)}), bf16[2,96,4096]{2,1,0:T(8,128)(2,1)}) %all-reduce.40.cloned.1.call-update) | async-done | bytes 1572880 | tf_op jit(solution)/shard_map/psum | solution.py:170
  167.1 2.4 fusion.29
  169.5 2.5 collective-permute-start.1
  172.0 19.5 %collective-permute-done.1 = bf16[2,96,4096]{2,1,0:T(8,128)(2,1)S(1)} collective-permute-done((bf16[2,96,4096]{2,1,0:T(8,128)(2,1)S(1)}, bf16[2,96,4096]{2,1,0:T(8,128)(2,1)S(1)}, u32[]{:S(2)}, u32[]{:S(2)}) %collective-permute-start.1) | collective-permute-done | bytes 1572896 | tf_op jit(solution)/shard_map/ppermute | solution.py:16
  195.5 2.2 fusion.132
  197.9 4.5 convolution_convert_fusion.1
  202.5 50.4 %all-reduce.42.cloned.1.call-done = bf16[2,96,4096]{2,1,0:T(8,128)(2,1)} async-done(((bf16[2,96,4096]{2,1,0:T(8,128)(2,1)}), bf16[2,96,4096]{2,1,0:T(8,128)(2,1)}) %all-reduce.42.cloned.1.call-update) | async-done | bytes 1572880 | tf_op jit(solution)/shard_map/psum | solution.py:170
  252.9 3.1 fusion.33
  258.0 20.1 %collective-permute-done.2 = bf16[2,96,4096]{2,1,0:T(8,128)(2,1)} collective-permute-done((bf16[2,96,4096]{2,1,0:T(8,128)(2,1)}, bf16[2,96,4096]{2,1,0:T(8,128)(2,1)}, u32[]{:S(2)}, u32[]{:S(2)}) %collective-permute-start.2) | collective-permute-done | bytes 1572896 | tf_op jit(solution)/shard_map/ppermute | solution.py:16
  278.1 3.7 fusion.44
  282.6 2.5 copy-done.43
  291.8 2.2 fusion.133
  294.3 4.5 convolution_convert_fusion
  302.4 46.9 %all-reduce.44.cloned.1.call-done = bf16[2,96,4096]{2,1,0:T(8,128)(2,1)} async-done(((bf16[2,96,4096]{2,1,0:T(8,128)(2,1)}), bf16[2,96,4096]{2,1,0:T(8,128)(2,1)}) %all-reduce.44.cloned.1.call-update) | async-done | bytes 1572880 | tf_op jit(solution)/shard_map/psum | solution.py:170
  349.3 4.7 fusion.68
  354.1 34.6 %all-gather.1 = bf16[8,2,4096]{2,1,0:T(2,128)(2,1)S(1)} all-gather(bf16[1,2,4096]{2,1,0:T(2,128)(2,1)S(1)} %fusion.387), channel_id=2, replica_groups=mesh['section'=4,'dp'=8,'mp'=4] {'dp'}, dimensions={0}, use_global_device_ids=true | all-gather | bytes 147456 | tf_op jit(solution)/shard_map/all_gather | solution.py:244
  402.0 2.2 fusion.105
  414.3 50.1 %all-reduce.46.cloned.1.call-done = bf16[2,96,4096]{2,1,0:T(8,128)(2,1)} async-done(((bf16[2,96,4096]{2,1,0:T(8,128)(2,1)}), bf16[2,96,4096]{2,1,0:T(8,128)(2,1)}) %all-reduce.46.cloned.1.call-update) | async-done | bytes 1572880 | tf_op jit(solution)/shard_map/psum | solution.py:196
  468.4 2.2 collective-permute-start.3
  470.6 17.7 %collective-permute-done.3 = bf16[2,96,4096]{2,1,0:T(8,128)(2,1)S(1)} collective-permute-done((bf16[2,96,4096]{2,1,0:T(8,128)(2,1)S(1)}, bf16[2,96,4096]{2,1,0:T(8,128)(2,1)S(1)}, u32[]{:S(2)}, u32[]{:S(2)}) %collective-permute-start.3) | collective-permute-done | bytes 1572896 | tf_op jit(solution)/shard_map/ppermute | solution.py:16
  504.3 51.8 %all-reduce.48.cloned.1.call-done = bf16[2,96,4096]{2,1,0:T(8,128)(2,1)} async-done(((bf16[2,96,4096]{2,1,0:T(8,128)(2,1)}), bf16[2,96,4096]{2,1,0:T(8,128)(2,1)}) %all-reduce.48.cloned.1.call-update) | async-done | bytes 1572880 | tf_op jit(solution)/shard_map/psum | solution.py:196
  561.8 17.9 %collective-permute-done.4 = bf16[2,96,4096]{2,1,0:T(8,128)(2,1)S(1)} collective-permute-done((bf16[2,96,4096]{2,1,0:T(8,128)(2,1)S(1)}, bf16[2,96,4096]{2,1,0:T(8,128)(2,1)S(1)}, u32[]{:S(2)}, u32[]{:S(2)}) %collective-permute-start.4) | collective-permute-done | bytes 1572896 | tf_op jit(solution)/shard_map/ppermute | solution.py:16
  582.7 2.3 fusion.111
  596.1 51.6 %all-reduce.50.cloned.1.call-done = bf16[2,96,4096]{2,1,0:T(8,128)(2,1)} async-done(((bf16[2,96,4096]{2,1,0:T(8,128)(2,1)}), bf16[2,96,4096]{2,1,0:T(8,128)(2,1)}) %all-reduce.50.cloned.1.call-update) | async-done | bytes 1572880 | tf_op jit(solution)/shard_map/psum | solution.py:196
  657.7 13.8 %collective-permute-done.5 = bf16[2,96,4096]{2,1,0:T(8,128)(2,1)S(1)} collective-permute-done((bf16[2,96,4096]{2,1,0:T(8,128)(2,1)S(1)}, bf16[2,96,4096]{2,1,0:T(8,128)(2,1)S(1)}, u32[]{:S(2)}, u32[]{:S(2)}) %collective-permute-start.5) | collective-permute-done | bytes 1572896 | tf_op jit(solution)/shard_map/ppermute | solution.py:16
  673.3 2.2 fusion.114
  685.3 6.5 all-to-all-start.2
  692.1 4.4 copy.230
  706.9 7.5 all-to-all-start.1
  715.0 2.4 copy.227
  717.4 6.9 fusion.66
  725.4 7.7 all-to-all-start
  733.1 2.4 fusion.658
  735.5 7.5 all-to-all-done
  742.9 16.8 %all_to_all.26 = bf16[8,96,512]{2,1,0:T(8,128)(2,1)} all-to-all(bf16[8,96,512]{2,1,0:T(8,128)(2,1)S(1)} %get-tuple-element.62), channel_id=1, replica_groups=mesh['section'=4,'dp'=8,'mp'=4] {'dp'}, dimensions={0} | all-to-all | bytes 1572864 | tf_op jit(solution)/shard_map/all_to_all | solution.py:47
  759.8 6.2 all-to-all-start.3
  772.8 4.3 all-to-all-done.3
  777.0 2.6 pad_maximum_fusion.1
  779.7 3.2 fusion.61
  784.8 3.4 fusion.97
  (497 shorter events, 129.1 us)
Async XLA Ops:
  7.2 14.1 %copy-start = (bf16[1,4096,128]{2,1,0:T(8,128)(2,1)S(1)}, bf16[1,4096,128]{2,1,0:T(8,128)(2,1)}, u32[]{:S(2)}) copy-start(bf16[1,4096,128]{2,1,0:T(8,128)(2,1)} %param.14) | copy-start | bytes 3145732
  7.2 72.1 %all-reduce.38.cloned.1.call-start = ((), (), s32[]{:S(2)}) async-start(), calls=%async_computation.5 | async-start | bytes 3145728 | tf_op jit(solution)/shard_map/psum | solution.py:170
  7.3 292.7 %copy-start.70 = (pred[96,96]{0,1:T(8,128)(4,1)}, pred[96,96]{0,1:T(8,128)(4,1)S(1)}, u32[]{:S(2)}) copy-start(pred[96,96]{0,1:T(8,128)(4,1)S(1)} %iota_compare_fusion) | copy-start | bytes 27652
  9.2 6.8 copy-start.9
  9.2 6.8 copy-start.58
  26.7 140.4 %all-reduce.40.cloned.1.call-start = ((), (), s32[]{:S(2)}) async-start(), calls=%async_computation.6 | async-start | bytes 3145728 | tf_op jit(solution)/shard_map/psum | solution.py:170
  82.4 22.0 %collective-permute-start = (bf16[2,96,4096]{2,1,0:T(8,128)(2,1)}, bf16[2,96,4096]{2,1,0:T(8,128)(2,1)}, u32[]{:S(2)}, u32[]{:S(2)}) collective-permute-start(bf16[2,96,4096]{2,1,0:T(8,128)(2,1)} %fusion.25), channel_id=1, source_target_pairs={{0,32},{32,64},{64,96},{1,33},{33,65},{65,97},{2,34},{34,66},{66,9... | collective-permute-start | bytes 4718600 | tf_op jit(solution)/shard_map/ppermute | solution.py:16
  84.3 22.3 %copy-start.41 = (bf16[512,4096]{1,0:T(8,128)(2,1)S(1)}, bf16[512,4096]{1,0:T(8,128)(2,1)}, u32[]{:S(2)}) copy-start(bf16[512,4096]{1,0:T(8,128)(2,1)} %copy.215) | copy-start | bytes 12582916
  116.6 136.3 %all-reduce.42.cloned.1.call-start = ((), (), s32[]{:S(2)}) async-start(), calls=%async_computation.7 | async-start | bytes 3145728 | tf_op jit(solution)/shard_map/psum | solution.py:170
  169.5 22.8 %copy-start.54 = (bf16[2,96,4096]{2,1,0:T(8,128)(2,1)}, bf16[2,96,4096]{2,1,0:T(8,128)(2,1)S(1)}, u32[]{:S(2)}) copy-start(bf16[2,96,4096]{2,1,0:T(8,128)(2,1)S(1)} %fusion.29) | copy-start | bytes 4718596
  169.5 22.8 %copy-start.42 = (bf16[512,4096]{1,0:T(8,128)(2,1)S(1)}, bf16[512,4096]{1,0:T(8,128)(2,1)}, u32[]{:S(2)}) copy-start(bf16[512,4096]{1,0:T(8,128)(2,1)} %copy.215) | copy-start | bytes 12582916
  169.5 22.0 %collective-permute-start.1 = (bf16[2,96,4096]{2,1,0:T(8,128)(2,1)S(1)}, bf16[2,96,4096]{2,1,0:T(8,128)(2,1)S(1)}, u32[]{:S(2)}, u32[]{:S(2)}) collective-permute-start(bf16[2,96,4096]{2,1,0:T(8,128)(2,1)S(1)} %fusion.29), channel_id=1, source_target_pairs={{0,32},{32,64},{64,96},{1,33},{33,65},{65,97},{2,34},{34,66},{66,9... | collective-permute-start | bytes 4718600 | tf_op jit(solution)/shard_map/ppermute | solution.py:16
  197.9 55.0 %copy-start.24 = (bf16[2,96,4096]{2,1,0:T(8,128)(2,1)S(1)}, bf16[2,96,4096]{2,1,0:T(8,128)(2,1)}, u32[]{:S(2)}) copy-start(bf16[2,96,4096]{2,1,0:T(8,128)(2,1)} %copy-done.23) | copy-start | bytes 4718596
  202.4 146.9 %all-reduce.44.cloned.1.call-start = ((), (), s32[]{:S(2)}) async-start(), calls=%async_computation.8 | async-start | bytes 3145728 | tf_op jit(solution)/shard_map/psum | solution.py:170
  256.0 22.0 %collective-permute-start.2 = (bf16[2,96,4096]{2,1,0:T(8,128)(2,1)}, bf16[2,96,4096]{2,1,0:T(8,128)(2,1)}, u32[]{:S(2)}, u32[]{:S(2)}) collective-permute-start(bf16[2,96,4096]{2,1,0:T(8,128)(2,1)} %fusion.33), channel_id=1, source_target_pairs={{0,32},{32,64},{64,96},{1,33},{33,65},{65,97},{2,34},{34,66},{66,9... | collective-permute-start | bytes 4718600 | tf_op jit(solution)/shard_map/ppermute | solution.py:16
  281.8 7.1 copy-start.40
  294.2 5.4 copy-start.96
  294.2 5.4 copy-start.97
  294.2 5.5 copy-start.62
  294.3 5.5 copy-start.63
  298.8 165.7 %all-reduce.46.cloned.1.call-start = ((), (), s32[]{:S(2)}) async-start(), calls=%async_computation.9 | async-start | bytes 3145728 | tf_op jit(solution)/shard_map/psum | solution.py:196
  299.0 55.0 %copy-start.120 = (f32[2]{0:T(128)}, f32[2]{0:T(128)S(1)}, u32[]{:S(2)}) copy-start(f32[2]{0:T(128)S(1)} %fusion.646) | copy-start | bytes 28
  299.9 107.5 %copy-start.64 = (bf16[2,96,4,128]{3,1,2,0:T(8,128)(2,1)}, bf16[2,96,4,128]{3,1,2,0:T(8,128)(2,1)S(1)}, u32[]{:S(2)}) copy-start(bf16[2,96,4,128]{3,1,2,0:T(8,128)(2,1)S(1)} %pad_maximum_fusion.3) | copy-start | bytes 589828
  300.2 107.2 %copy-start.98 = (f32[2,4,96]{2,1,0:T(4,128)}, f32[2,4,96]{2,1,0:T(4,128)S(1)}, u32[]{:S(2)}) copy-start(f32[2,4,96]{2,1,0:T(4,128)S(1)} %get-tuple-element.182) | copy-start | bytes 9220
  300.4 53.6 %copy-start.113 = (f32[2,4,96]{2,1,0:T(4,128)}, f32[2,4,96]{2,1,0:T(4,128)S(1)}, u32[]{:S(2)}) copy-start(f32[2,4,96]{2,1,0:T(4,128)S(1)} %fusion.647) | copy-start | bytes 9220
  300.4 105.5 %copy-start.100 = (f32[2,4,96]{2,1,0:T(4,128)}, f32[2,4,96]{2,1,0:T(4,128)S(1)}, u32[]{:S(2)}) copy-start(f32[2,4,96]{2,1,0:T(4,128)S(1)} %multiply_divide_fusion) | copy-start | bytes 9220
  302.4 103.5 %copy-start.55 = (bf16[2,96,128,1]{2,1,3,0:T(8,128)(2,1)}, bf16[2,96,128,1]{2,1,3,0:T(8,128)(2,1)S(1)}, u32[]{:S(2)}) copy-start(bf16[2,96,128,1]{2,1,3,0:T(8,128)(2,1)S(1)} %fusion.152) | copy-start | bytes 147460
  349.3 42.8 %copy-start.112 = (s32[8]{0:T(128)S(1)}, s32[8]{0:T(128)}, u32[]{:S(2)}) copy-start(s32[8]{0:T(128)} %param.10) | copy-start | bytes 100
  388.7 13.1 %copy-start.121 = (f32[2]{0:T(128)S(1)}, f32[2]{0:T(128)}, u32[]{:S(2)}) copy-start(f32[2]{0:T(128)} %copy-done.120) | copy-start | bytes 28
  388.7 13.2 %copy-start.5 = (bf16[1,512,4096]{2,1,0:T(8,128)(2,1)S(1)}, bf16[1,512,4096]{2,1,0:T(8,128)(2,1)}, u32[]{:S(2)}) copy-start(bf16[1,512,4096]{2,1,0:T(8,128)(2,1)} %param.15) | copy-start | bytes 12582916
  388.7 13.2 %copy-start.102 = (f32[2,96]{1,0:T(2,128)S(1)}, f32[2,96]{1,0:T(2,128)}, u32[]{:S(2)}) copy-start(f32[2,96]{1,0:T(2,128)} %get-tuple-element.123) | copy-start | bytes 2308
  414.3 141.8 %all-reduce.48.cloned.1.call-start = ((), (), s32[]{:S(2)}) async-start(), calls=%async_computation.10 | async-start | bytes 3145728 | tf_op jit(solution)/shard_map/psum | solution.py:196
  467.2 24.1 %copy-start.6 = (bf16[1,512,4096]{2,1,0:T(8,128)(2,1)S(1)}, bf16[1,512,4096]{2,1,0:T(8,128)(2,1)}, u32[]{:S(2)}) copy-start(bf16[1,512,4096]{2,1,0:T(8,128)(2,1)} %param.15) | copy-start | bytes 12582916
  468.4 20.0 %collective-permute-start.3 = (bf16[2,96,4096]{2,1,0:T(8,128)(2,1)S(1)}, bf16[2,96,4096]{2,1,0:T(8,128)(2,1)S(1)}, u32[]{:S(2)}, u32[]{:S(2)}) collective-permute-start(bf16[2,96,4096]{2,1,0:T(8,128)(2,1)S(1)} %fusion.42), channel_id=1, source_target_pairs={{32,0},{64,32},{96,64},{33,1},{65,33},{97,65},{34,2},{66,34},{98,6... | collective-permute-start | bytes 4718600 | tf_op jit(solution)/shard_map/ppermute | solution.py:16
  504.3 143.4 %all-reduce.50.cloned.1.call-start = ((), (), s32[]{:S(2)}) async-start(), calls=%async_computation.11 | async-start | bytes 3145728 | tf_op jit(solution)/shard_map/psum | solution.py:196
  558.5 24.2 %copy-start.7 = (bf16[1,512,4096]{2,1,0:T(8,128)(2,1)S(1)}, bf16[1,512,4096]{2,1,0:T(8,128)(2,1)}, u32[]{:S(2)}) copy-start(bf16[1,512,4096]{2,1,0:T(8,128)(2,1)} %param.15) | copy-start | bytes 12582916
  559.9 19.8 %collective-permute-start.4 = (bf16[2,96,4096]{2,1,0:T(8,128)(2,1)S(1)}, bf16[2,96,4096]{2,1,0:T(8,128)(2,1)S(1)}, u32[]{:S(2)}, u32[]{:S(2)}) collective-permute-start(bf16[2,96,4096]{2,1,0:T(8,128)(2,1)S(1)} %fusion.39), channel_id=1, source_target_pairs={{32,0},{64,32},{96,64},{33,1},{65,33},{97,65},{34,2},{66,34},{98,6... | collective-permute-start | bytes 4718600 | tf_op jit(solution)/shard_map/ppermute | solution.py:16
  595.9 183.8 %all-gather.4.cloned.1.call-start = ((), (), s32[]{:S(2)}) async-start(), calls=%async_computation.12 | async-start | bytes 4423680 | tf_op jit(solution)/shard_map/all_gather | solution.py:57
  650.1 5.6 copy-start.47
  650.1 5.6 copy-start.49
  651.6 20.0 %collective-permute-start.5 = (bf16[2,96,4096]{2,1,0:T(8,128)(2,1)S(1)}, bf16[2,96,4096]{2,1,0:T(8,128)(2,1)S(1)}, u32[]{:S(2)}, u32[]{:S(2)}) collective-permute-start(bf16[2,96,4096]{2,1,0:T(8,128)(2,1)S(1)} %fusion.41), channel_id=1, source_target_pairs={{32,0},{64,32},{96,64},{33,1},{65,33},{97,65},{34,2},{66,34},{98,6... | collective-permute-start | bytes 4718600 | tf_op jit(solution)/shard_map/ppermute | solution.py:16
  655.7 17.5 %copy-start.8 = (bf16[1,512,4096]{2,1,0:T(8,128)(2,1)S(1)}, bf16[1,512,4096]{2,1,0:T(8,128)(2,1)}, u32[]{:S(2)}) copy-start(bf16[1,512,4096]{2,1,0:T(8,128)(2,1)} %param.15) | copy-start | bytes 12582916
  673.2 5.3 copy-start.72
  685.3 21.6 %all-to-all-start.2 = ((bf16[8,96,512]{2,1,0:T(8,128)(2,1)}), bf16[8,96,512]{2,1,0:T(8,128)(2,1)}, u32[]{:S(2)}, u32[]{:S(2)}) async-start(bf16[8,96,512]{2,1,0:T(8,128)(2,1)} %get-tuple-element.66), calls=%async_computation.2 | async-start | bytes 1572864 | tf_op jit(solution)/shard_map/all_to_all | solution.py:47
  706.9 10.6 %copy-start.39 = (bf16[24,8,8,512]{3,2,1,0:T(8,128)(2,1)S(1)}, bf16[24,8,8,512]{3,2,1,0:T(8,128)(2,1)}, u32[]{:S(2)}) copy-start(bf16[24,8,8,512]{3,2,1,0:T(8,128)(2,1)} %copy.229) | copy-start | bytes 4718596
  706.9 18.5 %all-to-all-start.1 = ((bf16[8,96,512]{2,1,0:T(8,128)(2,1)}), bf16[8,96,512]{2,1,0:T(8,128)(2,1)S(1)}, u32[]{:S(2)}, u32[]{:S(2)}) async-start(bf16[8,96,512]{2,1,0:T(8,128)(2,1)} %get-tuple-element.65), calls=%async_computation.1 | async-start | bytes 1572864 | tf_op jit(solution)/shard_map/all_to_all | solution.py:47
  725.4 17.6 %all-to-all-start = ((f32[32,1,128]{2,1,0:T(1,128)}), f32[32,1,128]{2,1,0:T(1,128)S(1)}, u32[]{:S(2)}, u32[]{:S(2)}) async-start(f32[32,1,128]{2,1,0:T(1,128)} %bitcast.213), calls=%async_computation | async-start | bytes 32768 | tf_op jit(solution)/shard_map/all_to_all | solution.py:26
  759.8 17.2 %all-to-all-start.3 = ((bf16[8,96,512]{2,1,0:T(8,128)(2,1)}), bf16[8,96,512]{2,1,0:T(8,128)(2,1)}, u32[]{:S(2)}, u32[]{:S(2)}) async-start(bf16[8,96,512]{2,1,0:T(8,128)(2,1)} %get-tuple-element.61), calls=%async_computation.3 | async-start | bytes 1572864 | tf_op jit(solution)/shard_map/all_to_all | solution.py:47
  (93 other events, 240.8 us)
Sparse Core Ops, SparseCore 0:
  26.8 52.4 all-reduce.37
  116.8 50.2 all-reduce.39
  202.6 50.3 all-reduce.41
  298.9 50.3 all-reduce.43
  414.4 49.9 all-reduce.45
  504.4 51.6 all-reduce.47
  596.0 51.6 all-reduce.49
  681.5 85.7 all-gather.3
where the time goes:
time: 805 us; the launch traced here: 795 us
  waiting for transfers between devices  476 us (59%)
  matrix products  95.4 us (12%)
  other arithmetic  58.7 us (7%)
  local copies, waits for them, and re-layouts  51.7 us (6%)
  blocking collectives  51.5 us (6%)
  starting transfers between devices  40.9 us (5%)
  between operations  21.1 us (3%)
    psum x4, waiting for transfers between devices, forward_section(): lax.psum(partial_value.astype(jnp.bfloat16), 'mp').astype(jnp.float32)  200 us
    psum x3, waiting for transfers between devices, backward_section(): lax.psum(member_grad.astype(jnp.bfloat16), 'mp').astype(jnp.float32)  154 us
    ppermute x6, waiting for transfers between devices, passed_along(): lax.ppermute(value, axis, [(source, source + steps) for source in range(f...  109 us
    all_gather x1, blocking collectives, local(): lax.all_gather(pooled.astype(jnp.bfloat16), 'dp', axis=0, tiled=True)  34.6 us
    unnamed x256, local copies, waits for them, and re-layouts  30.1 us
    dot_general x16, matrix products, contract_last(): lax.dot_general(left, right, (((left.ndim - 1,), (1,)), ((), ())), prefer...  23.3 us
    all_to_all x3, starting transfers between devices, exchange_in_pieces(): lax.all_to_all(piece, axis, split_axis=0, concat_axis=0, tiled=True)  20.2 us
    dot_general x4, matrix products, forward_section(): jnp.dot(mixture, out_weight, preferred_element_type=jnp.float32)  17.6 us
  transfers between devices with their start and end apart: 18, of which 16 were waited for; matrix products, arithmetic and copies ran while one was open for 5% of the time, Pallas kernels for 0%

commit v1 on v0

--- a/solution.py
+++ b/solution.py
@@ -167,7 +167,9 @@
         jnp.dot(normed, value_weight, preferred_element_type=jnp.float32),
     ).astype(jnp.bfloat16)
     partial_value = jnp.dot(mixture, out_weight, preferred_element_type=jnp.float32)
-    total_value = lax.psum(partial_value.astype(jnp.bfloat16), "mp").astype(jnp.float32)
+    total_value = jnp.sum(lax.all_gather(partial_value.astype(jnp.bfloat16), "mp"), axis=0).astype(
+        jnp.float32
+    )
     return (hidden_f + total_value).astype(jnp.bfloat16)
 
 

time: 805 us -> 890 us (1.11)
  waiting for transfers between devices: 476 us -> 538 us
  other arithmetic: 58.7 us -> 81.2 us
    all_gather x0 -> x4, waiting for transfers between devices: none -> 263 us  [forward_section(): lax.all_gather(partial_value.astype(jnp.bfloat16), 'mp')]
    psum x4 -> x0, waiting for transfers between devices: 200 us -> none  [forward_section(): lax.psum(partial_value.astype(jnp.bfloat16), 'mp').astype(jnp.float32)]
    reduce_sum x0 -> x4, other arithmetic: none -> 22.5 us  [forward_section(): jnp.sum(lax.all_gather(partial_value.astype(jnp.bfloat16), 'mp'), axis=0)]
where the time goes in v1:
time: 890 us; the launch traced here: 882 us
  waiting for transfers between devices  538 us (60%)
  matrix products  95.2 us (11%)
  other arithmetic  81.2 us (9%)
  blocking collectives  54.2 us (6%)
  local copies, waits for them, and re-layouts  51.7 us (6%)
  starting transfers between devices  41.1 us (5%)
  between operations  21.2 us (2%)
    all_gather x4, waiting for transfers between devices, forward_section(): lax.all_gather(partial_value.astype(jnp.bfloat16), 'mp')  263 us
    psum x3, waiting for transfers between devices, backward_section(): lax.psum(member_grad.astype(jnp.bfloat16), 'mp').astype(jnp.float32)  154 us
    ppermute x6, waiting for transfers between devices, passed_along(): lax.ppermute(value, axis, [(source, source + steps) for source in range(f...  108 us
    all_gather x1, blocking collectives, local(): lax.all_gather(pooled.astype(jnp.bfloat16), 'dp', axis=0, tiled=True)  34.3 us
    unnamed x256, local copies, waits for them, and re-layouts  30.1 us
    dot_general x16, matrix products, contract_last(): lax.dot_general(left, right, (((left.ndim - 1,), (1,)), ((), ())), prefer...  23.3 us
    reduce_sum x4, other arithmetic, forward_section(): jnp.sum(lax.all_gather(partial_value.astype(jnp.bfloat16), 'mp'), axis=0)  22.5 us
    all_to_all x1, blocking collectives, exchange_in_pieces(): lax.all_to_all(piece, axis, split_axis=0, concat_axis=0, tiled=True)  19.9 us
  transfers between devices with their start and end apart: 18, of which 16 were waited for; matrix products, arithmetic and copies ran while one was open for 5% of the time, Pallas kernels for 0%

profile of v1, /device:TPU:32, one launch (start us, length us, event | category | flops | bytes accessed | tf_op | source)
XLA Modules:
  0.0 882.2 jit_solution(14673104632840676197)
XLA Ops:
  9.2 6.5 copy.215
  15.9 3.8 fusion.80
  22.3 4.3 convolution_convert_fusion.3
  26.7 67.8 %all-gather.14.cloned.1.call-done = bf16[8,96,4096]{2,1,0:T(8,128)(2,1)} async-done(((bf16[2,96,4096]{2,1,0:T(8,128)(2,1)}), bf16[8,96,4096]{2,1,0:T(8,128)(2,1)}) %all-gather.14.cloned.1.call-update) | async-done | bytes 6291472 | tf_op jit(solution)/shard_map/all_gather | solution.py:170
  94.5 5.6 reduce_sum.688
  100.1 3.1 fusion.25
  103.2 2.4 collective-permute-start
  105.7 19.6 %collective-permute-done = bf16[2,96,4096]{2,1,0:T(8,128)(2,1)} collective-permute-done((bf16[2,96,4096]{2,1,0:T(8,128)(2,1)}, bf16[2,96,4096]{2,1,0:T(8,128)(2,1)}, u32[]{:S(2)}, u32[]{:S(2)}) %collective-permute-start) | collective-permute-done | bytes 1572896 | tf_op jit(solution)/shard_map/ppermute | solution.py:16
  133.1 4.3 convolution_convert_fusion.2
  137.4 66.2 %all-gather.16.cloned.1.call-done = bf16[8,96,4096]{2,1,0:T(8,128)(2,1)} async-done(((bf16[2,96,4096]{2,1,0:T(8,128)(2,1)}), bf16[8,96,4096]{2,1,0:T(8,128)(2,1)}) %all-gather.16.cloned.1.call-update) | async-done | bytes 6291472 | tf_op jit(solution)/shard_map/all_gather | solution.py:170
  203.7 5.6 reduce_sum.694
  209.3 2.4 fusion.29
  211.7 2.5 collective-permute-start.1
  214.2 19.5 %collective-permute-done.1 = bf16[2,96,4096]{2,1,0:T(8,128)(2,1)S(1)} collective-permute-done((bf16[2,96,4096]{2,1,0:T(8,128)(2,1)S(1)}, bf16[2,96,4096]{2,1,0:T(8,128)(2,1)S(1)}, u32[]{:S(2)}, u32[]{:S(2)}) %collective-permute-start.1) | collective-permute-done | bytes 1572896 | tf_op jit(solution)/shard_map/ppermute | solution.py:16
  240.1 4.3 convolution_convert_fusion.1
  244.5 66.2 %all-gather.18.cloned.1.call-done = bf16[8,96,4096]{2,1,0:T(8,128)(2,1)} async-done(((bf16[2,96,4096]{2,1,0:T(8,128)(2,1)}), bf16[8,96,4096]{2,1,0:T(8,128)(2,1)}) %all-gather.18.cloned.1.call-update) | async-done | bytes 6291472 | tf_op jit(solution)/shard_map/all_gather | solution.py:170
  310.8 5.7 reduce_sum.700
  316.5 3.1 fusion.33
  321.8 19.9 %collective-permute-done.2 = bf16[2,96,4096]{2,1,0:T(8,128)(2,1)} collective-permute-done((bf16[2,96,4096]{2,1,0:T(8,128)(2,1)}, bf16[2,96,4096]{2,1,0:T(8,128)(2,1)}, u32[]{:S(2)}, u32[]{:S(2)}) %collective-permute-start.2) | collective-permute-done | bytes 1572896 | tf_op jit(solution)/shard_map/ppermute | solution.py:16
  341.7 3.7 fusion.44
  346.2 2.5 copy-done.43
  357.9 4.4 convolution_convert_fusion
  366.3 62.3 %all-gather.20.cloned.1.call-done = bf16[8,96,4096]{2,1,0:T(8,128)(2,1)} async-done(((bf16[2,96,4096]{2,1,0:T(8,128)(2,1)}), bf16[8,96,4096]{2,1,0:T(8,128)(2,1)}) %all-gather.20.cloned.1.call-update) | async-done | bytes 6291472 | tf_op jit(solution)/shard_map/all_gather | solution.py:170
  428.6 5.6 reduce_sum.706
  434.2 4.7 fusion.68
  439.0 34.3 %all-gather.5 = bf16[8,2,4096]{2,1,0:T(2,128)(2,1)S(1)} all-gather(bf16[1,2,4096]{2,1,0:T(2,128)(2,1)S(1)} %fusion.387), channel_id=6, replica_groups=mesh['section'=4,'dp'=8,'mp'=4] {'dp'}, dimensions={0}, use_global_device_ids=true | all-gather | bytes 147456 | tf_op jit(solution)/shard_map/all_gather | solution.py:246
  499.1 50.5 %all-reduce.34.cloned.1.call-done = bf16[2,96,4096]{2,1,0:T(8,128)(2,1)} async-done(((bf16[2,96,4096]{2,1,0:T(8,128)(2,1)}), bf16[2,96,4096]{2,1,0:T(8,128)(2,1)}) %all-reduce.34.cloned.1.call-update) | async-done | bytes 1572880 | tf_op jit(solution)/shard_map/psum | solution.py:198
  555.6 17.9 %collective-permute-done.3 = bf16[2,96,4096]{2,1,0:T(8,128)(2,1)S(1)} collective-permute-done((bf16[2,96,4096]{2,1,0:T(8,128)(2,1)S(1)}, bf16[2,96,4096]{2,1,0:T(8,128)(2,1)S(1)}, u32[]{:S(2)}, u32[]{:S(2)}) %collective-permute-start.3) | collective-permute-done | bytes 1572896 | tf_op jit(solution)/shard_map/ppermute | solution.py:16
  589.5 51.8 %all-reduce.36.cloned.1.call-done = bf16[2,96,4096]{2,1,0:T(8,128)(2,1)} async-done(((bf16[2,96,4096]{2,1,0:T(8,128)(2,1)}), bf16[2,96,4096]{2,1,0:T(8,128)(2,1)}) %all-reduce.36.cloned.1.call-update) | async-done | bytes 1572880 | tf_op jit(solution)/shard_map/psum | solution.py:198
  647.2 17.7 %collective-permute-done.4 = bf16[2,96,4096]{2,1,0:T(8,128)(2,1)S(1)} collective-permute-done((bf16[2,96,4096]{2,1,0:T(8,128)(2,1)S(1)}, bf16[2,96,4096]{2,1,0:T(8,128)(2,1)S(1)}, u32[]{:S(2)}, u32[]{:S(2)}) %collective-permute-start.4) | collective-permute-done | bytes 1572896 | tf_op jit(solution)/shard_map/ppermute | solution.py:16
  667.9 2.3 fusion.111
  681.1 51.8 %all-reduce.38.cloned.1.call-done = bf16[2,96,4096]{2,1,0:T(8,128)(2,1)} async-done(((bf16[2,96,4096]{2,1,0:T(8,128)(2,1)}), bf16[2,96,4096]{2,1,0:T(8,128)(2,1)}) %all-reduce.38.cloned.1.call-update) | async-done | bytes 1572880 | tf_op jit(solution)/shard_map/psum | solution.py:198
  736.8 2.3 collective-permute-start.5
  743.2 13.5 %collective-permute-done.5 = bf16[2,96,4096]{2,1,0:T(8,128)(2,1)S(1)} collective-permute-done((bf16[2,96,4096]{2,1,0:T(8,128)(2,1)S(1)}, bf16[2,96,4096]{2,1,0:T(8,128)(2,1)S(1)}, u32[]{:S(2)}, u32[]{:S(2)}) %collective-permute-start.5) | collective-permute-done | bytes 1572896 | tf_op jit(solution)/shard_map/ppermute | solution.py:16
  770.5 6.5 all-to-all-start.2
  777.3 4.4 copy.230
  792.1 7.6 all-to-all-start.1
  800.3 2.4 copy.227
  802.7 6.9 fusion.66
  810.7 7.6 all-to-all-start
  818.4 2.4 fusion.658
  820.8 7.3 all-to-all-done
  828.1 19.9 %all_to_all.26 = bf16[8,96,512]{2,1,0:T(8,128)(2,1)} all-to-all(bf16[8,96,512]{2,1,0:T(8,128)(2,1)S(1)} %get-tuple-element.62), channel_id=1, replica_groups=mesh['section'=4,'dp'=8,'mp'=4] {'dp'}, dimensions={0} | all-to-all | bytes 1572864 | tf_op jit(solution)/shard_map/all_to_all | solution.py:47
  848.0 4.9 all-to-all-start.3
  859.9 4.1 all-to-all-done.3
  864.0 2.6 pad_maximum_fusion.1
  866.6 3.2 fusion.61
  871.8 3.4 fusion.97
  (501 shorter events, 139.3 us)
Async XLA Ops:
  7.2 14.1 %copy-start = (bf16[1,4096,128]{2,1,0:T(8,128)(2,1)S(1)}, bf16[1,4096,128]{2,1,0:T(8,128)(2,1)}, u32[]{:S(2)}) copy-start(bf16[1,4096,128]{2,1,0:T(8,128)(2,1)} %param.14) | copy-start | bytes 3145732
  7.2 87.3 %all-gather.14.cloned.1.call-start = ((), (), s32[]{:S(2)}) async-start(), calls=%async_computation.9 | async-start | bytes 7864320 | tf_op jit(solution)/shard_map/all_gather | solution.py:170
  7.3 356.6 %copy-start.70 = (pred[96,96]{0,1:T(8,128)(4,1)}, pred[96,96]{0,1:T(8,128)(4,1)S(1)}, u32[]{:S(2)}) copy-start(pred[96,96]{0,1:T(8,128)(4,1)S(1)} %iota_compare_fusion) | copy-start | bytes 27652
  9.2 6.8 copy-start.9
  9.2 6.8 copy-start.58
  26.6 177.1 %all-gather.16.cloned.1.call-start = ((), (), s32[]{:S(2)}) async-start(), calls=%async_computation.10 | async-start | bytes 7864320 | tf_op jit(solution)/shard_map/all_gather | solution.py:170
  103.2 22.0 %collective-permute-start = (bf16[2,96,4096]{2,1,0:T(8,128)(2,1)}, bf16[2,96,4096]{2,1,0:T(8,128)(2,1)}, u32[]{:S(2)}, u32[]{:S(2)}) collective-permute-start(bf16[2,96,4096]{2,1,0:T(8,128)(2,1)} %fusion.25), channel_id=1, source_target_pairs={{0,32},{32,64},{64,96},{1,33},{33,65},{65,97},{2,34},{34,66},{66,9... | collective-permute-start | bytes 4718600 | tf_op jit(solution)/shard_map/ppermute | solution.py:16
  105.6 21.7 %copy-start.41 = (bf16[512,4096]{1,0:T(8,128)(2,1)S(1)}, bf16[512,4096]{1,0:T(8,128)(2,1)}, u32[]{:S(2)}) copy-start(bf16[512,4096]{1,0:T(8,128)(2,1)} %copy.215) | copy-start | bytes 12582916
  137.4 173.4 %all-gather.18.cloned.1.call-start = ((), (), s32[]{:S(2)}) async-start(), calls=%async_computation.11 | async-start | bytes 7864320 | tf_op jit(solution)/shard_map/all_gather | solution.py:170
  211.7 22.8 %copy-start.54 = (bf16[2,96,4096]{2,1,0:T(8,128)(2,1)}, bf16[2,96,4096]{2,1,0:T(8,128)(2,1)S(1)}, u32[]{:S(2)}) copy-start(bf16[2,96,4096]{2,1,0:T(8,128)(2,1)S(1)} %fusion.29) | copy-start | bytes 4718596
  211.7 22.8 %copy-start.42 = (bf16[512,4096]{1,0:T(8,128)(2,1)S(1)}, bf16[512,4096]{1,0:T(8,128)(2,1)}, u32[]{:S(2)}) copy-start(bf16[512,4096]{1,0:T(8,128)(2,1)} %copy.215) | copy-start | bytes 12582916
  211.7 22.0 %collective-permute-start.1 = (bf16[2,96,4096]{2,1,0:T(8,128)(2,1)S(1)}, bf16[2,96,4096]{2,1,0:T(8,128)(2,1)S(1)}, u32[]{:S(2)}, u32[]{:S(2)}) collective-permute-start(bf16[2,96,4096]{2,1,0:T(8,128)(2,1)S(1)} %fusion.29), channel_id=1, source_target_pairs={{0,32},{32,64},{64,96},{1,33},{33,65},{65,97},{2,34},{34,66},{66,9... | collective-permute-start | bytes 4718600 | tf_op jit(solution)/shard_map/ppermute | solution.py:16
  244.5 184.1 %all-gather.20.cloned.1.call-start = ((), (), s32[]{:S(2)}) async-start(), calls=%async_computation.12 | async-start | bytes 7864320 | tf_op jit(solution)/shard_map/all_gather | solution.py:170
  310.8 5.7 copy-start.24
  319.6 22.0 %collective-permute-start.2 = (bf16[2,96,4096]{2,1,0:T(8,128)(2,1)}, bf16[2,96,4096]{2,1,0:T(8,128)(2,1)}, u32[]{:S(2)}, u32[]{:S(2)}) collective-permute-start(bf16[2,96,4096]{2,1,0:T(8,128)(2,1)} %fusion.33), channel_id=1, source_target_pairs={{0,32},{32,64},{64,96},{1,33},{33,65},{65,97},{2,34},{34,66},{66,9... | collective-permute-start | bytes 4718600 | tf_op jit(solution)/shard_map/ppermute | solution.py:16
  345.4 7.1 copy-start.40
  357.8 5.8 copy-start.96
  357.8 5.8 copy-start.97
  357.8 5.9 copy-start.62
  357.9 5.9 copy-start.63
  362.3 187.3 %all-reduce.34.cloned.1.call-start = ((), (), s32[]{:S(2)}) async-start(), calls=%async_computation.5 | async-start | bytes 3145728 | tf_op jit(solution)/shard_map/psum | solution.py:198
  363.0 75.9 %copy-start.120 = (f32[2]{0:T(128)}, f32[2]{0:T(128)S(1)}, u32[]{:S(2)}) copy-start(f32[2]{0:T(128)S(1)} %fusion.646) | copy-start | bytes 28
  363.9 128.3 %copy-start.64 = (bf16[2,96,4,128]{3,1,2,0:T(8,128)(2,1)}, bf16[2,96,4,128]{3,1,2,0:T(8,128)(2,1)S(1)}, u32[]{:S(2)}) copy-start(bf16[2,96,4,128]{3,1,2,0:T(8,128)(2,1)S(1)} %pad_maximum_fusion.3) | copy-start | bytes 589828
  364.2 128.0 %copy-start.98 = (f32[2,4,96]{2,1,0:T(4,128)}, f32[2,4,96]{2,1,0:T(4,128)S(1)}, u32[]{:S(2)}) copy-start(f32[2,4,96]{2,1,0:T(4,128)S(1)} %get-tuple-element.182) | copy-start | bytes 9220
  364.3 69.9 %copy-start.113 = (f32[2,4,96]{2,1,0:T(4,128)}, f32[2,4,96]{2,1,0:T(4,128)S(1)}, u32[]{:S(2)}) copy-start(f32[2,4,96]{2,1,0:T(4,128)S(1)} %fusion.647) | copy-start | bytes 9220
  364.3 126.2 %copy-start.100 = (f32[2,4,96]{2,1,0:T(4,128)}, f32[2,4,96]{2,1,0:T(4,128)S(1)}, u32[]{:S(2)}) copy-start(f32[2,4,96]{2,1,0:T(4,128)S(1)} %multiply_divide_fusion) | copy-start | bytes 9220
  366.3 124.2 %copy-start.55 = (bf16[2,96,128,1]{2,1,3,0:T(8,128)(2,1)}, bf16[2,96,128,1]{2,1,3,0:T(8,128)(2,1)S(1)}, u32[]{:S(2)}) copy-start(bf16[2,96,128,1]{2,1,3,0:T(8,128)(2,1)S(1)} %fusion.152) | copy-start | bytes 147460
  434.2 42.4 %copy-start.112 = (s32[8]{0:T(128)S(1)}, s32[8]{0:T(128)}, u32[]{:S(2)}) copy-start(s32[8]{0:T(128)} %param.10) | copy-start | bytes 100
  473.3 13.2 %copy-start.121 = (f32[2]{0:T(128)S(1)}, f32[2]{0:T(128)}, u32[]{:S(2)}) copy-start(f32[2]{0:T(128)} %copy-done.120) | copy-start | bytes 28
  473.3 13.3 %copy-start.5 = (bf16[1,512,4096]{2,1,0:T(8,128)(2,1)S(1)}, bf16[1,512,4096]{2,1,0:T(8,128)(2,1)}, u32[]{:S(2)}) copy-start(bf16[1,512,4096]{2,1,0:T(8,128)(2,1)} %param.15) | copy-start | bytes 12582916
  473.3 13.3 %copy-start.102 = (f32[2,96]{1,0:T(2,128)S(1)}, f32[2,96]{1,0:T(2,128)}, u32[]{:S(2)}) copy-start(f32[2,96]{1,0:T(2,128)} %get-tuple-element.123) | copy-start | bytes 2308
  498.9 142.4 %all-reduce.36.cloned.1.call-start = ((), (), s32[]{:S(2)}) async-start(), calls=%async_computation.6 | async-start | bytes 3145728 | tf_op jit(solution)/shard_map/psum | solution.py:198
  552.3 24.1 %copy-start.6 = (bf16[1,512,4096]{2,1,0:T(8,128)(2,1)S(1)}, bf16[1,512,4096]{2,1,0:T(8,128)(2,1)}, u32[]{:S(2)}) copy-start(bf16[1,512,4096]{2,1,0:T(8,128)(2,1)} %param.15) | copy-start | bytes 12582916
  553.5 20.0 %collective-permute-start.3 = (bf16[2,96,4096]{2,1,0:T(8,128)(2,1)S(1)}, bf16[2,96,4096]{2,1,0:T(8,128)(2,1)S(1)}, u32[]{:S(2)}, u32[]{:S(2)}) collective-permute-start(bf16[2,96,4096]{2,1,0:T(8,128)(2,1)S(1)} %fusion.42), channel_id=1, source_target_pairs={{32,0},{64,32},{96,64},{33,1},{65,33},{97,65},{34,2},{66,34},{98,6... | collective-permute-start | bytes 4718600 | tf_op jit(solution)/shard_map/ppermute | solution.py:16
  589.5 143.5 %all-reduce.38.cloned.1.call-start = ((), (), s32[]{:S(2)}) async-start(), calls=%async_computation.7 | async-start | bytes 3145728 | tf_op jit(solution)/shard_map/psum | solution.py:198
  643.7 24.2 %copy-start.7 = (bf16[1,512,4096]{2,1,0:T(8,128)(2,1)S(1)}, bf16[1,512,4096]{2,1,0:T(8,128)(2,1)}, u32[]{:S(2)}) copy-start(bf16[1,512,4096]{2,1,0:T(8,128)(2,1)} %param.15) | copy-start | bytes 12582916
  645.1 19.8 %collective-permute-start.4 = (bf16[2,96,4096]{2,1,0:T(8,128)(2,1)S(1)}, bf16[2,96,4096]{2,1,0:T(8,128)(2,1)S(1)}, u32[]{:S(2)}, u32[]{:S(2)}) collective-permute-start(bf16[2,96,4096]{2,1,0:T(8,128)(2,1)S(1)} %fusion.39), channel_id=1, source_target_pairs={{32,0},{64,32},{96,64},{33,1},{65,33},{97,65},{34,2},{66,34},{98,6... | collective-permute-start | bytes 4718600 | tf_op jit(solution)/shard_map/ppermute | solution.py:16
  681.1 185.6 %all-gather.12.cloned.1.call-start = ((), (), s32[]{:S(2)}) async-start(), calls=%async_computation.8 | async-start | bytes 4423680 | tf_op jit(solution)/shard_map/all_gather | solution.py:57
  735.3 5.9 copy-start.47
  735.3 5.9 copy-start.49
  736.7 5.5 copy-start.51
  736.8 20.0 %collective-permute-start.5 = (bf16[2,96,4096]{2,1,0:T(8,128)(2,1)S(1)}, bf16[2,96,4096]{2,1,0:T(8,128)(2,1)S(1)}, u32[]{:S(2)}, u32[]{:S(2)}) collective-permute-start(bf16[2,96,4096]{2,1,0:T(8,128)(2,1)S(1)} %fusion.41), channel_id=1, source_target_pairs={{32,0},{64,32},{96,64},{33,1},{65,33},{97,65},{34,2},{66,34},{98,6... | collective-permute-start | bytes 4718600 | tf_op jit(solution)/shard_map/ppermute | solution.py:16
  741.2 17.2 %copy-start.8 = (bf16[1,512,4096]{2,1,0:T(8,128)(2,1)S(1)}, bf16[1,512,4096]{2,1,0:T(8,128)(2,1)}, u32[]{:S(2)}) copy-start(bf16[1,512,4096]{2,1,0:T(8,128)(2,1)} %param.15) | copy-start | bytes 12582916
  770.5 21.6 %all-to-all-start.2 = ((bf16[8,96,512]{2,1,0:T(8,128)(2,1)}), bf16[8,96,512]{2,1,0:T(8,128)(2,1)}, u32[]{:S(2)}, u32[]{:S(2)}) async-start(bf16[8,96,512]{2,1,0:T(8,128)(2,1)} %get-tuple-element.66), calls=%async_computation.2 | async-start | bytes 1572864 | tf_op jit(solution)/shard_map/all_to_all | solution.py:47
  792.1 10.6 %copy-start.39 = (bf16[24,8,8,512]{3,2,1,0:T(8,128)(2,1)S(1)}, bf16[24,8,8,512]{3,2,1,0:T(8,128)(2,1)}, u32[]{:S(2)}) copy-start(bf16[24,8,8,512]{3,2,1,0:T(8,128)(2,1)} %copy.229) | copy-start | bytes 4718596
  792.1 18.6 %all-to-all-start.1 = ((bf16[8,96,512]{2,1,0:T(8,128)(2,1)}), bf16[8,96,512]{2,1,0:T(8,128)(2,1)S(1)}, u32[]{:S(2)}, u32[]{:S(2)}) async-start(bf16[8,96,512]{2,1,0:T(8,128)(2,1)} %get-tuple-element.65), calls=%async_computation.1 | async-start | bytes 1572864 | tf_op jit(solution)/shard_map/all_to_all | solution.py:47
  810.7 17.4 %all-to-all-start = ((f32[32,1,128]{2,1,0:T(1,128)}), f32[32,1,128]{2,1,0:T(1,128)S(1)}, u32[]{:S(2)}, u32[]{:S(2)}) async-start(f32[32,1,128]{2,1,0:T(1,128)} %bitcast.217), calls=%async_computation | async-start | bytes 32768 | tf_op jit(solution)/shard_map/all_to_all | solution.py:26
  848.0 16.0 %all-to-all-start.3 = ((bf16[8,96,512]{2,1,0:T(8,128)(2,1)}), bf16[8,96,512]{2,1,0:T(8,128)(2,1)}, u32[]{:S(2)}, u32[]{:S(2)}) async-start(bf16[8,96,512]{2,1,0:T(8,128)(2,1)} %get-tuple-element.61), calls=%async_computation.3 | async-start | bytes 1572864 | tf_op jit(solution)/shard_map/all_to_all | solution.py:47
  (93 other events, 242.2 us)
Sparse Core Ops, SparseCore 0:
  26.7 67.7 all-gather.13
  137.5 66.1 all-gather.15
  244.6 66.1 all-gather.17
  362.4 66.1 all-gather.19
  499.0 50.5 all-reduce.33
  589.6 51.6 all-reduce.35
  681.2 51.6 all-reduce.37
  766.7 83.9 all-gather.11
